TPU v7x, 32 devices: a whole 2x2x4 slice. The times are simulated.
32 devices in a mesh: grp: 16 (over z, x, core), uly: 2 (over y).
Axes of the slice: x: 2, y: 2, z: 4, core: 2. Of those that a mesh axis runs over, the one named last changes fastest.
Arguments:
- queries: bfloat16 [4096, 32, 128], P(('grp', 'uly')), may hold values from -16 to 16
- keys: bfloat16 [4096, 4, 128], P(('grp', 'uly')), may hold values from -8 to 8
- values: bfloat16 [4096, 4, 128], P(('grp', 'uly')), may hold values from -6 to 6
- output_cotangent: bfloat16 [4096, 32, 128], P(('grp', 'uly')), may hold values from -6 to 6
- block_lists: int32 [128, 1], replicated, may hold values from 0 to 127, as said below
- list_counts: int32 [128], replicated, may hold values from 0 to 1, as said below
Outputs:
- attended: bfloat16 [4096, 32, 128], P(('grp', 'uly'))
- query_grad: bfloat16 [4096, 32, 128], P(('grp', 'uly'))
- key_gradient: bfloat16 [4096, 4, 128], P(('grp', 'uly'))
- value_gradient: bfloat16 [4096, 4, 128], P(('grp', 'uly'))
Inputs may be any that keep to these rules, and one draw needn't show every extreme that they name: `block_lists`: calling an aligned run of 8 blocks a group: every entry of block b's list is a block of another group than b's, and the entries of all lists of one group, counted or not, lie in pairwise different groups. `list_counts`: some block counts all 1 entries in every draw.
All inputs are finite; a program needn't handle non-finite values.
Results may differ from a plain program's by a relative error of at most 0.039.
Values may be sent and summed in bfloat16 or wider, within the bound.
No kernel may reach another device: no remote copies, remote signals or barrier semaphores. Data moves between devices by JAX's collectives and lax.ppermute only.
A program may use at most 128 MiB of HBM per device.

v0:
```python
import jax
import jax.numpy as jnp
from jax import lax
from jax.sharding import PartitionSpec as P


def on_device(queries, keys, values, output_cotangent, block_lists, list_counts):
    uly_count = lax.axis_size("uly")
    grp_count = lax.axis_size("grp")
    my_group = lax.axis_index("grp")
    tokens, head_count, head_width = queries.shape
    kv_heads = keys.shape[1]
    copies = max(1, uly_count // kv_heads)
    blocks_all, remote = block_lists.shape
    per_group = blocks_all // grp_count
    block_tok = tokens * uly_count // per_group
    group_tok = tokens * uly_count
    score_scale = head_width ** (-0.5)
    lists = block_lists.reshape(grp_count, per_group, remote)
    counted = (jnp.arange(remote)[None, :] < list_counts[:, None]).reshape(
        grp_count, per_group, remote
    )
    wanted = (lists // per_group == my_group) & counted
    send_place = jnp.sum(jnp.where(wanted, lists % per_group, 0), axis=(1, 2))
    sending = jnp.any(wanted, axis=(1, 2))
    mine_source = lax.dynamic_index_in_dim(lists, my_group, 0, keepdims=False) // per_group
    mine_counted = lax.dynamic_index_in_dim(counted, my_group, 0, keepdims=False)
    trip_count = jnp.max(jnp.sum(mine_counted.astype(jnp.int32), axis=1))

    def to_blocks(array_in):
        return array_in.reshape((per_group, block_tok) + array_in.shape[1:])

    keys_wide = jnp.repeat(keys, copies, axis=1)
    values_wide = jnp.repeat(values, copies, axis=1)
    query_heads, grad_heads, key_heads, value_heads = (
        lax.all_to_all(queries, "uly", split_axis=1, concat_axis=0, tiled=True),
        lax.all_to_all(output_cotangent, "uly", split_axis=1, concat_axis=0, tiled=True),
        lax.all_to_all(keys_wide, "uly", split_axis=1, concat_axis=0, tiled=True),
        lax.all_to_all(values_wide, "uly", split_axis=1, concat_axis=0, tiled=True),
    )
    stacked = jnp.stack([to_blocks(key_heads), to_blocks(value_heads)])
    outgoing = jnp.take(stacked, send_place, axis=1)
    arrived = lax.all_to_all(outgoing, "grp", split_axis=1, concat_axis=1, tiled=True)
    kv_local = key_heads.shape[1]
    heads_local = query_heads.shape[1]
    heads_per_group = heads_local // kv_local
    query_blk = query_heads.reshape(per_group, block_tok, kv_local, heads_per_group, head_width)
    grad_blk = grad_heads.reshape(per_group, block_tok, kv_local, heads_per_group, head_width)
    key_blk = to_blocks(key_heads)
    value_blk = to_blocks(value_heads)
    far_keys = arrived[0]
    far_values = arrived[1]
    causal = jnp.arange(block_tok)[:, None] >= jnp.arange(block_tok)[None, :]

    def logits(key_rows):
        return (
            jnp.einsum("pqkgd,pjkd->pkgqj", query_blk, key_rows, preferred_element_type=jnp.float32)
            * score_scale
        )

    def slot_rows(slot_index):
        source = lax.dynamic_index_in_dim(mine_source, slot_index, 1, keepdims=False)
        counted_slot = lax.dynamic_index_in_dim(mine_counted, slot_index, 1, keepdims=False)
        return (
            jnp.take(far_keys, source, axis=0),
            jnp.take(far_values, source, axis=0),
            counted_slot,
            source,
        )

    def masked(scores, counted_slot):
        return jnp.where(counted_slot[:, None, None, None, None], scores, -jnp.inf)

    near_scores = jnp.where(causal, logits(key_blk), -jnp.inf)
    highest = jnp.max(near_scores, axis=-1)
    denominator = jnp.sum(jnp.exp(near_scores - highest[..., None]), axis=-1)

    def max_sweep(slot_index, state_pair):
        highest, denominator = state_pair
        key_rows, value_rows, counted_slot, source = slot_rows(slot_index)
        scores = masked(logits(key_rows), counted_slot)
        new_highest = jnp.maximum(highest, jnp.max(scores, axis=-1))
        denominator = denominator * jnp.exp(highest - new_highest) + jnp.sum(
            jnp.exp(scores - new_highest[..., None]), axis=-1
        )
        return (new_highest, denominator)

    highest, denominator = lax.fori_loop(0, trip_count, max_sweep, (highest, denominator))
    log_total = highest + jnp.log(denominator)

    def softmax_weights(scores):
        return jnp.exp(scores - log_total[..., None])

    summed = jnp.einsum(
        "pkgqj,pjkd->pqkgd",
        softmax_weights(near_scores).astype(jnp.bfloat16),
        value_blk,
        preferred_element_type=jnp.float32,
    )

    def value_sweep(slot_index, summed):
        key_rows, value_rows, counted_slot, source = slot_rows(slot_index)
        weights = softmax_weights(masked(logits(key_rows), counted_slot)).astype(jnp.bfloat16)
        return summed + jnp.einsum(
            "pkgqj,pjkd->pqkgd", weights, value_rows, preferred_element_type=jnp.float32
        )

    summed = lax.fori_loop(0, trip_count, value_sweep, summed)
    attended_blk = summed.astype(jnp.bfloat16)
    row_delta = jnp.transpose(
        jnp.sum(grad_blk.astype(jnp.float32) * attended_blk.astype(jnp.float32), axis=-1),
        (0, 2, 3, 1),
    )

    def backward(scores, key_rows, value_rows):
        probs = softmax_weights(scores)
        weights = probs.astype(jnp.bfloat16)
        dprobs = jnp.einsum(
            "pqkgd,pjkd->pkgqj", grad_blk, value_rows, preferred_element_type=jnp.float32
        )
        dscores = (probs * (dprobs - row_delta[..., None])).astype(jnp.bfloat16)
        query_term = jnp.einsum(
            "pkgqj,pjkd->pqkgd", dscores, key_rows, preferred_element_type=jnp.float32
        )
        key_term = (
            jnp.einsum("pkgqj,pqkgd->pjkd", dscores, query_blk, preferred_element_type=jnp.float32)
            * score_scale
        )
        value_term = jnp.einsum(
            "pkgqj,pqkgd->pjkd", weights, grad_blk, preferred_element_type=jnp.float32
        )
        return (query_term, key_term, value_term)

    query_sum, key_near, value_near = backward(near_scores, key_blk, value_blk)
    far_grads = jnp.zeros((2, grp_count, block_tok, kv_local, head_width), jnp.float32)

    def grad_sweep(slot_index, state_pair):
        query_sum, far_grads = state_pair
        key_rows, value_rows, counted_slot, source = slot_rows(slot_index)
        query_term, key_term, value_term = backward(
            masked(logits(key_rows), counted_slot), key_rows, value_rows
        )
        routing = (
            (source[:, None] == jnp.arange(grp_count)[None, :]) & counted_slot[:, None]
        ).astype(jnp.float32)
        routed = jnp.einsum(
            "ps,xpjkd->xsjkd",
            routing,
            jnp.stack([key_term, value_term]),
            precision=lax.Precision.HIGHEST,
        )
        return (query_sum + query_term, far_grads + routed)

    query_sum, far_grads = lax.fori_loop(0, trip_count, grad_sweep, (query_sum, far_grads))
    owners = ((send_place[:, None] == jnp.arange(per_group)[None, :]) & sending[:, None]).astype(
        jnp.float32
    )
    returned = lax.all_to_all(far_grads, "grp", split_axis=1, concat_axis=1, tiled=True)
    landed = jnp.einsum("sp,xsjkd->xpjkd", owners, returned, precision=lax.Precision.HIGHEST)
    key_local = (key_near + landed[0]).reshape(group_tok, kv_local, head_width)
    value_local = (value_near + landed[1]).reshape(group_tok, kv_local, head_width)
    attended_rows = attended_blk.reshape(group_tok, heads_local, head_width)
    query_rows = (
        (query_sum * score_scale).astype(jnp.bfloat16).reshape(group_tok, heads_local, head_width)
    )
    attended, query_grad = (
        lax.all_to_all(attended_rows, "uly", split_axis=0, concat_axis=1, tiled=True),
        lax.all_to_all(query_rows, "uly", split_axis=0, concat_axis=1, tiled=True),
    )
    key_parts, value_parts = (
        lax.all_to_all(key_local, "uly", split_axis=0, concat_axis=1, tiled=True),
        lax.all_to_all(value_local, "uly", split_axis=0, concat_axis=1, tiled=True),
    )
    key_gradient = jnp.sum(key_parts.reshape(tokens, kv_heads, copies, head_width), axis=2).astype(
        jnp.bfloat16
    )
    value_gradient = jnp.sum(
        value_parts.reshape(tokens, kv_heads, copies, head_width), axis=2
    ).astype(jnp.bfloat16)
    return (attended, query_grad, key_gradient, value_gradient)


def solution(mesh):
    placed = (
        P(("grp", "uly"), None, None),
        P(("grp", "uly"), None, None),
        P(("grp", "uly"), None, None),
        P(("grp", "uly"), None, None),
        P(),
        P(),
    )
    return jax.shard_map(
        on_device,
        mesh=mesh,
        in_specs=placed,
        out_specs=(
            P(("grp", "uly"), None, None),
            P(("grp", "uly"), None, None),
            P(("grp", "uly"), None, None),
            P(("grp", "uly"), None, None),
        ),
        check_vma=False,
    )
```

profile of v0, /device:TPU:0, one launch (start us, length us, event | category | flops | bytes accessed | tf_op | source)
XLA Modules:
  0.0 215.2 jit_solution(12773727700696270377)
XLA Ops:
  2.3 4.2 %all-to-all-start = ((bf16[128,4,128]{2,0,1:T(8,128)(2,1)}), bf16[128,4,128]{2,0,1:T(8,128)(2,1)S(1)}, u32[]{:S(2)}, u32[]{:S(2)}) async-start(bf16[128,4,128]{2,0,1:T(8,128)(2,1)} %copy.88), calls=%async_computation | async-start | bytes 262144 | tf_op jit(solution)/shard_map/all_to_all | solution.py:38
  11.4 2.6 %copy.90 = bf16[128,32,128]{2,0,1:T(8,128)(2,1)} copy(bf16[128,32,128]{2,1,0:T(8,128)(2,1)} %param.14) | data formatting | bytes 2097152 | tf_op args[0]
  15.4 3.4 %all-to-all-start.2 = ((bf16[128,4,128]{2,0,1:T(8,128)(2,1)}), bf16[128,4,128]{2,0,1:T(8,128)(2,1)S(1)}, u32[]{:S(2)}, u32[]{:S(2)}) async-start(bf16[128,4,128]{2,0,1:T(8,128)(2,1)} %copy.96), calls=%async_computation.2 | async-start | bytes 262144 | tf_op jit(solution)/shard_map/all_to_all | solution.py:39
  18.9 4.4 %all-to-all-done.2 = bf16[128,4,128]{2,0,1:T(8,128)(2,1)S(1)} async-done(((bf16[128,4,128]{2,0,1:T(8,128)(2,1)}), bf16[128,4,128]{2,0,1:T(8,128)(2,1)S(1)}, u32[]{:S(2)}, u32[]{:S(2)}) %all-to-all-start.2) | async-done | bytes 131104 | tf_op jit(solution)/shard_map/all_to_all | solution.py:39
  23.4 3.6 %all-to-all-start.1 = ((bf16[128,32,128]{2,0,1:T(8,128)(2,1)}), bf16[128,32,128]{2,0,1:T(8,128)(2,1)S(1)}, u32[]{:S(2)}, u32[]{:S(2)}) async-start(bf16[128,32,128]{2,0,1:T(8,128)(2,1)} %copy.90), calls=%async_computation.1 | async-start | bytes 2097152 | tf_op jit(solution)/shard_map/all_to_all | solution.py:36
  27.0 12.9 %all-to-all-done.1 = bf16[128,32,128]{2,0,1:T(8,128)(2,1)S(1)} async-done(((bf16[128,32,128]{2,0,1:T(8,128)(2,1)}), bf16[128,32,128]{2,0,1:T(8,128)(2,1)S(1)}, u32[]{:S(2)}, u32[]{:S(2)}) %all-to-all-start.1) | async-done | bytes 1048608 | tf_op jit(solution)/shard_map/all_to_all | solution.py:36
  39.9 3.6 %all-to-all-start.5 = ((bf16[128,32,128]{2,0,1:T(8,128)(2,1)}), bf16[128,32,128]{2,0,1:T(8,128)(2,1)S(1)}, u32[]{:S(2)}, u32[]{:S(2)}) async-start(bf16[128,32,128]{2,0,1:T(8,128)(2,1)} %copy.108), calls=%async_computation.5 | async-start | bytes 2097152 | tf_op jit(solution)/shard_map/all_to_all | solution.py:37
  45.9 9.7 %all-to-all-done.5 = bf16[128,32,128]{2,0,1:T(8,128)(2,1)S(1)} async-done(((bf16[128,32,128]{2,0,1:T(8,128)(2,1)}), bf16[128,32,128]{2,0,1:T(8,128)(2,1)S(1)}, u32[]{:S(2)}, u32[]{:S(2)}) %all-to-all-start.5) | async-done | bytes 1048608 | tf_op jit(solution)/shard_map/all_to_all | solution.py:37
  55.6 5.9 %all-to-all-start.3 = ((bf16[2,16,32,2,128]{4,2,3,0,1:T(8,128)(2,1)}), bf16[2,16,32,2,128]{4,2,3,0,1:T(8,128)(2,1)}, u32[]{:S(2)}, u32[]{:S(2)}) async-start(bf16[2,16,32,2,128]{4,2,3,0,1:T(8,128)(2,1)} %select_bitcast_fusion), calls=%async_computation.3 | async-start | bytes 1048576 | tf_op jit(solution)/shard_map/all_to_all | solution.py:43
  62.3 2.3 %copy.110 = bf16[2,128,16,128]{3,2,1,0:T(8,128)(2,1)S(1)} copy(bf16[2,128,16,128]{3,1,2,0:T(8,128)(2,1)} %bitcast.255) | data formatting | bytes 2097152 | tf_op jit(solution)/shard_map/all_to_all | solution.py:37
  69.0 7.0 %all-to-all-done.3 = bf16[2,16,32,2,128]{4,2,3,0,1:T(8,128)(2,1)} async-done(((bf16[2,16,32,2,128]{4,2,3,0,1:T(8,128)(2,1)}), bf16[2,16,32,2,128]{4,2,3,0,1:T(8,128)(2,1)}, u32[]{:S(2)}, u32[]{:S(2)}) %all-to-all-start.3) | async-done | bytes 524320 | tf_op jit(solution)/shard_map/all_to_all | solution.py:43
  81.5 3.0 %copy.101 = f32[8,2,32,32,8]{3,4,2,1,0:T(8,128)} copy(f32[8,2,32,32,8]{3,2,4,1,0:T(8,128)S(1)} %fusion.57) | data formatting | bytes 1048576 | tf_op jit(solution)/shard_map/while | solution.py:88
  86.4 4.7 %while.43 = (s32[]{:T(128)}, f32[8,2,8,32]{3,2,1,0:T(8,128)S(1)}, f32[8,2,8,32]{3,2,1,0:T(8,128)}, s32[]{:T(128)}, pred[8,1]{0,1:T(4,128)(4,1)S(1)}, /*index=5*/f32[8,2,32,32,8]{3,4,2,1,0:T(8,128)}, s32[]{:T(128)}) while((s32[]{:T(128)}, f32[8,2,8,32]{3,2,1,0:T(8,128)S(1)}, f32[8,2,8,32]{3,2,1,0:T(8,128)}, s32[]{:T(128)}, ...), condition=%wide.region_7.9_spmd, body=%wide.region_4.8_spmd.sunk | while | flops 925698 | bytes 3489969 | solution.py:88
  92.0 3.5 %convolution_bitcast_fusion.1 = f32[8,32,2,8,128]{4,1,3,2,0:T(8,128)} fusion(f32[8,2,8,32,32]{3,4,2,1,0:T(8,128)} %copy-done.2, f32[8,2,8,32]{3,2,1,0:T(8,128)S(1)} %log_add_fusion, bf16[8,32,2,128,1]{3,1,0,2,4:T(8,128)(2,1)} %bitcast.260), kind=kOutput, calls=%fused_computation.52 | convolution fusion | flops 33816576 | bytes 2768896 | tf_op jit(solution)/shard_map/pkgqj,pjkd->pqkgd/dot_general | solution.py:94
  95.5 4.7 %while.44 = (s32[]{:T(128)}, f32[8,32,2,8,128]{4,1,3,2,0:T(8,128)}, s32[]{:T(128)}, pred[8,1]{0,1:T(4,128)(4,1)S(1)}, f32[8,2,32,32,8]{2,3,4,1,0:T(8,128)S(1)}, ...) while((s32[]{:T(128)}, f32[8,32,2,8,128]{4,1,3,2,0:T(8,128)}, s32[]{:T(128)}, ...), condition=%wide.region_9.11_spmd, body=%wide.region_8.10_spmd.sunk | while | flops 34603008 | bytes 4866141 | solution.py:108
  96.1 3.3 %bitcast_add_fusion.6 = f32[8,32,2,8,128]{4,1,3,2,0:T(8,128)} fusion(f32[8,32,2,8,128]{4,1,3,2,0:T(8,128)} %get-tuple-element.814, f32[8,2,32,32,8]{2,3,4,1,0:T(8,128)S(1)} %get-tuple-element.825, f32[8,2,8,32]{3,2,1,0:T(8,128)S(1)} %get-tuple-element.826, pred[8]{0:T(512)(128)(4,1)S(1)} %bitcast.277, bf16[8,32,2,128]{3,1,2,0:T(8,128)(2,1)S(1)} %get-tuple-element.827), kind=kOutput, calls=%fused_computation.9.clone.1 | convolution fusion | flops 34603008 | bytes 4866056 | tf_op jit(solution)/shard_map/while/body/pkgqj,pjkd->pqkgd/dot_general | solution.py:104
  100.2 3.1 %fusion.52 = f32[8,2,32,32,8]{3,2,4,1,0:T(8,128)} fusion(bf16[8,32,2,8,128]{4,3,2,1,0:T(8,128)(2,1)S(1)} %bitcast.243, bf16[8,32,2,128]{3,1,2,0:T(8,128)(2,1)S(1)} %get-tuple-element.868), kind=kOutput, calls=%fused_computation.76 | convolution fusion | flops 33554432 | bytes 1703936 | tf_op jit(solution)/shard_map/while/body/pqkgd,pjkd->pkgqj/dot_general | solution.py:118
  103.4 3.2 %multiply_reduce_fusion = (f32[8,32,2,8]{3,2,1,0:T(2,128)}, bf16[8,32,2,8,128]{4,3,2,1,0:T(8,128)(2,1)}) fusion(bf16[8,32,2,8,128]{4,3,2,1,0:T(8,128)(2,1)S(1)} %bitcast.244, f32[8,32,2,8,128]{4,1,3,2,0:T(8,128)S(1)} %copy-done.1), kind=kLoop, calls=%fused_computation.47 | loop fusion | flops 2093056 | bytes 4210688 | tf_op jit(solution)/shard_map/reduce_sum | solution.py:111
  107.6 3.3 %convolution_bitcast_fusion.4 = f32[1,8,32,2,128]{4,2,3,1,0:T(8,128)} fusion(f32[8,2,32,32,8]{3,2,4,1,0:T(8,128)} %copy-done.8, f32[8,2,8,32]{3,2,1,0:T(8,128)S(1)} %get-tuple-element.866, pred[8]{0:T(512)(128)(4,1)S(1)} %get-tuple-element.627, bf16[8,32,2,8,128]{4,3,2,1,0:T(8,128)(2,1)S(1)} %bitcast.245), kind=kOutput, calls=%fused_computation.56 | convolution fusion | flops 34078720 | bytes 1851400 | tf_op jit(solution)/shard_map/while/body/pkgqj,pqkgd->pjkd/dot_general | solution.py:129
  110.9 2.8 %fusion.28 = bf16[8,2,8,32,32]{3,4,2,1,0:T(8,128)(2,1)} fusion(f32[8,2,8,32,32]{3,4,2,1,0:T(8,128)S(1)} %copy-done.3, f32[8,2,8,32]{3,2,1,0:T(8,128)S(1)} %copy.113, f32[8,2,8,32]{3,2,1,0:T(8,128)S(1)} %get-tuple-element.866, bf16[8,32,2,8,128]{4,3,2,1,0:T(8,128)(2,1)S(1)} %bitcast.246, bf16[8,32,2,128,1]{3,1,0,2,4:T(8,128)(2,1)S(1)} %bitcast.261), kind=kOutput, calls=%fused_computation.42 | convolution fusion | flops 34078720 | bytes 1998848 | tf_op jit(solution)/shard_map/pqkgd,pjkd->pkgqj/dot_general | solution.py:118
  114.7 2.9 %copy.121 = f32[8,2,32,32,8]{2,3,4,1,0:T(8,128)} copy(f32[8,2,32,32,8]{3,2,4,1,0:T(8,128)} %fusion.52) | data formatting | bytes 1048576 | tf_op jit(solution)/shard_map/while | solution.py:154
  122.4 6.0 %while.45 = (s32[]{:T(128)}, f32[8,32,2,8,128]{4,1,3,2,0:T(8,128)}, f32[2,16,32,2,128]{4,3,2,1,0:T(2,128)S(1)}, s32[]{:T(128)}, pred[8,1]{0,1:T(4,128)(4,1)S(1)}...) while((s32[]{:T(128)}, f32[8,32,2,8,128]{4,1,3,2,0:T(8,128)}, ...), condition=%wide.region_12.14_spmd, body=%wide.region_11.13_spmd.sunk | while | flops 35127296 | bytes 12746905 | solution.py:154
  123.1 4.1 %bitcast_add_fusion.7 = f32[8,32,2,8,128]{4,1,3,2,0:T(8,128)} fusion(f32[8,32,2,8,128]{4,1,3,2,0:T(8,128)} %get-tuple-element.842, f32[8,2,32,32,8]{2,3,4,1,0:T(8,128)} %get-tuple-element.860, f32[8,2,32,32,8]{2,3,4,1,0:T(8,128)S(1)} %get-tuple-element.858, f32[8,2,8,32]{3,2,1,0:T(8,128)S(1)} %get-tuple-element.861, ...), kind=kOutput, calls=%fused_computation.20.clone.1 | convolution fusion | flops 34865152 | bytes 5406728 | tf_op jit(solution)/shard_map/while/body/pkgqj,pjkd->pqkgd/dot_general | solution.py:122
  128.4 4.0 %fusion.29 = bf16[8,32,2,8,128]{4,3,2,1,0:T(8,128)(2,1)} fusion(f32[8,32,2,8,128]{4,1,3,2,0:T(8,128)} %get-tuple-element.466), kind=kLoop, calls=%fused_computation.45 | loop fusion | flops 1048576 | bytes 3145728 | tf_op jit(solution)/shard_map/convert_element_type | solution.py:164
  132.4 3.6 %all-to-all-start.6 = ((bf16[256,16,128]{2,1,0:T(8,128)(2,1)}), bf16[256,16,128]{2,1,0:T(8,128)(2,1)S(1)}, u32[]{:S(2)}, u32[]{:S(2)}) async-start(bf16[256,16,128]{2,1,0:T(8,128)(2,1)} %bitcast.69), calls=%async_computation.6 | async-start | bytes 2097152 | tf_op jit(solution)/shard_map/all_to_all | solution.py:168
  136.1 13.9 %all-to-all-done.6 = bf16[256,16,128]{2,1,0:T(8,128)(2,1)S(1)} async-done(((bf16[256,16,128]{2,1,0:T(8,128)(2,1)}), bf16[256,16,128]{2,1,0:T(8,128)(2,1)S(1)}, u32[]{:S(2)}, u32[]{:S(2)}) %all-to-all-start.6) | async-done | bytes 1048608 | tf_op jit(solution)/shard_map/all_to_all | solution.py:168
  150.0 29.1 %all_to_all.124 = f32[2,16,32,2,128]{4,3,2,0,1:T(2,128)} all-to-all(f32[2,16,32,2,128]{4,3,2,0,1:T(2,128)S(1)} %copy.127), channel_id=1, replica_groups=mesh['grp'=16,'uly'=2] {'grp'}, dimensions={1} | all-to-all | bytes 2097152 | tf_op jit(solution)/shard_map/all_to_all | solution.py:158
  179.1 4.9 %all-to-all-start.4 = ((bf16[256,16,128]{2,1,0:T(8,128)(2,1)}), bf16[256,16,128]{2,1,0:T(8,128)(2,1)}, u32[]{:S(2)}, u32[]{:S(2)}) async-start(bf16[256,16,128]{2,1,0:T(8,128)(2,1)} %bitcast.252), calls=%async_computation.4 | async-start | bytes 2097152 | tf_op jit(solution)/shard_map/all_to_all | solution.py:167
  188.1 10.6 %all-to-all-done.4 = bf16[256,16,128]{2,1,0:T(8,128)(2,1)} async-done(((bf16[256,16,128]{2,1,0:T(8,128)(2,1)}), bf16[256,16,128]{2,1,0:T(8,128)(2,1)}, u32[]{:S(2)}, u32[]{:S(2)}) %all-to-all-start.4) | async-done | bytes 1048608 | tf_op jit(solution)/shard_map/all_to_all | solution.py:167
  198.7 3.4 %all-to-all-start.9 = ((bf16[256,2,128]{2,1,0:T(2,128)(2,1)}), bf16[256,2,128]{2,1,0:T(2,128)(2,1)S(1)}, u32[]{:S(2)}, u32[]{:S(2)}) async-start(bf16[256,2,128]{2,1,0:T(2,128)(2,1)} %copy.136), calls=%async_computation.9 | async-start | bytes 262144 | tf_op jit(solution)/shard_map/all_to_all | solution.py:172
  206.6 3.4 %all-to-all-start.8 = ((bf16[256,2,128]{2,1,0:T(2,128)(2,1)}), bf16[256,2,128]{2,1,0:T(2,128)(2,1)S(1)}, u32[]{:S(2)}, u32[]{:S(2)}) async-start(bf16[256,2,128]{2,1,0:T(2,128)(2,1)} %copy.131), calls=%async_computation.8 | async-start | bytes 262144 | tf_op jit(solution)/shard_map/all_to_all | solution.py:171
  211.1 2.4 %copy.107 = bf16[128,2,16,128]{3,2,1,0:T(8,128)(2,1)} copy(bf16[128,2,16,128]{3,2,0,1:T(8,128)(2,1)} %bitcast.44) | data formatting | bytes 2097152 | tf_op jit(solution)/shard_map/all_to_all | solution.py:167
  (125 shorter events, 45.9 us)
Async XLA Ops:
  0.6 13.4 %copy-start.24 = (bf16[128,32,128]{2,1,0:T(8,128)(2,1)S(1)}, bf16[128,32,128]{2,1,0:T(8,128)(2,1)}, u32[]{:S(2)}) copy-start(bf16[128,32,128]{2,1,0:T(8,128)(2,1)} %param.17) | copy-start | bytes 3145732
  2.3 13.1 %all-to-all-start = ((bf16[128,4,128]{2,0,1:T(8,128)(2,1)}), bf16[128,4,128]{2,0,1:T(8,128)(2,1)S(1)}, u32[]{:S(2)}, u32[]{:S(2)}) async-start(bf16[128,4,128]{2,0,1:T(8,128)(2,1)} %copy.88), calls=%async_computation | async-start | bytes 262144 | tf_op jit(solution)/shard_map/all_to_all | solution.py:38
  15.4 7.9 %all-to-all-start.2 = ((bf16[128,4,128]{2,0,1:T(8,128)(2,1)}), bf16[128,4,128]{2,0,1:T(8,128)(2,1)S(1)}, u32[]{:S(2)}, u32[]{:S(2)}) async-start(bf16[128,4,128]{2,0,1:T(8,128)(2,1)} %copy.96), calls=%async_computation.2 | async-start | bytes 262144 | tf_op jit(solution)/shard_map/all_to_all | solution.py:39
  18.9 21.0 %copy-start.27 = (s32[16]{0:T(128)}, s32[16]{0:T(128)S(1)}, u32[]{:S(2)}) copy-start(s32[16]{0:T(128)S(1)} %fusion.72) | copy-start | bytes 196
  23.4 16.6 %all-to-all-start.1 = ((bf16[128,32,128]{2,0,1:T(8,128)(2,1)}), bf16[128,32,128]{2,0,1:T(8,128)(2,1)S(1)}, u32[]{:S(2)}, u32[]{:S(2)}) async-start(bf16[128,32,128]{2,0,1:T(8,128)(2,1)} %copy.90), calls=%async_computation.1 | async-start | bytes 2097152 | tf_op jit(solution)/shard_map/all_to_all | solution.py:36
  39.9 15.7 %all-to-all-start.5 = ((bf16[128,32,128]{2,0,1:T(8,128)(2,1)}), bf16[128,32,128]{2,0,1:T(8,128)(2,1)S(1)}, u32[]{:S(2)}, u32[]{:S(2)}) async-start(bf16[128,32,128]{2,0,1:T(8,128)(2,1)} %copy.108), calls=%async_computation.5 | async-start | bytes 2097152 | tf_op jit(solution)/shard_map/all_to_all | solution.py:37
  44.2 20.4 %copy-start.19 = (bf16[2,128,2,128]{3,1,0,2:T(8,128)(2,1)}, bf16[2,128,2,128]{3,1,0,2:T(8,128)(2,1)S(1)}, u32[]{:S(2)}) copy-start(bf16[2,128,2,128]{3,1,0,2:T(8,128)(2,1)S(1)} %copy.89) | copy-start | bytes 393220
  44.2 11.4 %copy-start.21 = (bf16[2,128,2,128]{3,1,0,2:T(8,128)(2,1)}, bf16[2,128,2,128]{3,1,0,2:T(8,128)(2,1)S(1)}, u32[]{:S(2)}) copy-start(bf16[2,128,2,128]{3,1,0,2:T(8,128)(2,1)S(1)} %copy.97) | copy-start | bytes 393220
  55.6 6.7 %copy-start.16 = (bf16[128,32,128]{2,0,1:T(8,128)(2,1)}, bf16[128,32,128]{2,0,1:T(8,128)(2,1)S(1)}, u32[]{:S(2)}) copy-start(bf16[128,32,128]{2,0,1:T(8,128)(2,1)S(1)} %all-to-all-done.5) | copy-start | bytes 3145732
  55.6 20.4 %all-to-all-start.3 = ((bf16[2,16,32,2,128]{4,2,3,0,1:T(8,128)(2,1)}), bf16[2,16,32,2,128]{4,2,3,0,1:T(8,128)(2,1)}, u32[]{:S(2)}, u32[]{:S(2)}) async-start(bf16[2,16,32,2,128]{4,2,3,0,1:T(8,128)(2,1)} %select_bitcast_fusion), calls=%async_computation.3 | async-start | bytes 1048576 | tf_op jit(solution)/shard_map/all_to_all | solution.py:43
  62.3 16.1 %copy-start.10 = (bf16[2,128,16,128]{3,2,1,0:T(8,128)(2,1)}, bf16[2,128,16,128]{3,2,1,0:T(8,128)(2,1)S(1)}, u32[]{:S(2)}) copy-start(bf16[2,128,16,128]{3,2,1,0:T(8,128)(2,1)S(1)} %copy.92) | copy-start | bytes 3145732
  64.6 46.3 %copy-start.6 = (bf16[2,128,16,128]{3,2,1,0:T(8,128)(2,1)}, bf16[2,128,16,128]{3,2,1,0:T(8,128)(2,1)S(1)}, u32[]{:S(2)}) copy-start(bf16[2,128,16,128]{3,2,1,0:T(8,128)(2,1)S(1)} %copy.110) | copy-start | bytes 3145732
  87.0 2.8 %copy-start.17 = (f32[8,2,8,32]{3,2,1,0:T(8,128)S(1)}, f32[8,2,8,32]{3,2,1,0:T(8,128)}, u32[]{:S(2)}) copy-start(f32[8,2,8,32]{3,2,1,0:T(8,128)} %get-tuple-element.793) | copy-start | bytes 49156 | tf_op jit(solution)/shard_map/while
  100.2 3.1 %copy-start.1 = (f32[8,32,2,8,128]{4,1,3,2,0:T(8,128)S(1)}, f32[8,32,2,8,128]{4,1,3,2,0:T(8,128)}, u32[]{:S(2)}) copy-start(f32[8,32,2,8,128]{4,1,3,2,0:T(8,128)} %get-tuple-element.465) | copy-start | bytes 6291460
  107.6 3.3 %copy-start.3 = (f32[8,2,8,32,32]{3,4,2,1,0:T(8,128)S(1)}, f32[8,2,8,32,32]{3,4,2,1,0:T(8,128)}, u32[]{:S(2)}) copy-start(f32[8,2,8,32,32]{3,4,2,1,0:T(8,128)} %copy-done.2) | copy-start | bytes 1572868
  107.6 3.3 %copy-start.22 = (bf16[2,128,2,128]{3,1,0,2:T(8,128)(2,1)S(1)}, bf16[2,128,2,128]{3,1,0,2:T(8,128)(2,1)}, u32[]{:S(2)}) copy-start(bf16[2,128,2,128]{3,1,0,2:T(8,128)(2,1)} %copy-done.21) | copy-start | bytes 393220
  107.6 6.1 %copy-start.12 = (f32[8,2,32,32,8]{3,2,4,1,0:T(8,128)S(1)}, f32[8,2,32,32,8]{3,2,4,1,0:T(8,128)}, u32[]{:S(2)}) copy-start(f32[8,2,32,32,8]{3,2,4,1,0:T(8,128)} %fusion.52) | copy-start | bytes 1572868
  110.9 2.8 %copy-start.9 = (f32[8,2,32,32,8]{3,2,4,1,0:T(8,128)S(1)}, f32[8,2,32,32,8]{3,2,4,1,0:T(8,128)}, u32[]{:S(2)}) copy-start(f32[8,2,32,32,8]{3,2,4,1,0:T(8,128)} %copy-done.8) | copy-start | bytes 1572868
  110.9 2.8 %copy-start.11 = (bf16[2,128,16,128]{3,2,1,0:T(8,128)(2,1)S(1)}, bf16[2,128,16,128]{3,2,1,0:T(8,128)(2,1)}, u32[]{:S(2)}) copy-start(bf16[2,128,16,128]{3,2,1,0:T(8,128)(2,1)} %copy-done.10) | copy-start | bytes 3145732
  114.7 2.9 %copy-start.25 = (f32[1,8,32,2,128]{4,2,3,1,0:T(8,128)S(1)}, f32[1,8,32,2,128]{4,2,3,1,0:T(8,128)}, u32[]{:S(2)}) copy-start(f32[1,8,32,2,128]{4,2,3,1,0:T(8,128)} %convolution_bitcast_fusion.4) | copy-start | bytes 786436
  117.7 2.4 %copy-start.13 = (bf16[8,2,8,32,32]{3,4,2,1,0:T(8,128)(2,1)S(1)}, bf16[8,2,8,32,32]{3,4,2,1,0:T(8,128)(2,1)}, u32[]{:S(2)}) copy-start(bf16[8,2,8,32,32]{3,4,2,1,0:T(8,128)(2,1)} %fusion.28) | copy-start | bytes 786436
  123.0 4.1 %copy-start.5 = (f32[2,32,2,128,16]{3,2,1,4,0:T(2,128)S(1)}, f32[2,32,2,128,16]{3,2,1,4,0:T(2,128)}, u32[]{:S(2)}) copy-start(f32[2,32,2,128,16]{3,2,1,4,0:T(2,128)} %get-tuple-element.863) | copy-start | bytes 3145732 | tf_op jit(solution)/shard_map/while
  132.4 17.6 %all-to-all-start.6 = ((bf16[256,16,128]{2,1,0:T(8,128)(2,1)}), bf16[256,16,128]{2,1,0:T(8,128)(2,1)S(1)}, u32[]{:S(2)}, u32[]{:S(2)}) async-start(bf16[256,16,128]{2,1,0:T(8,128)(2,1)} %bitcast.69), calls=%async_computation.6 | async-start | bytes 2097152 | tf_op jit(solution)/shard_map/all_to_all | solution.py:168
  136.1 48.0 %copy-start.26 = (pred[16]{0:T(512)(128)(4,1)S(1)}, pred[16]{0:T(512)(128)(4,1)}, u32[]{:S(2)}) copy-start(pred[16]{0:T(512)(128)(4,1)} %get-tuple-element.620) | copy-start | bytes 52
  136.1 48.0 %copy-start.28 = (s32[16]{0:T(128)S(1)}, s32[16]{0:T(128)}, u32[]{:S(2)}) copy-start(s32[16]{0:T(128)} %copy-done.27) | copy-start | bytes 196
  150.0 29.1 %copy-start.14 = (bf16[256,16,128]{2,1,0:T(8,128)(2,1)}, bf16[256,16,128]{2,1,0:T(8,128)(2,1)S(1)}, u32[]{:S(2)}) copy-start(bf16[256,16,128]{2,1,0:T(8,128)(2,1)S(1)} %all-to-all-done.6) | copy-start | bytes 3145732
  179.1 7.4 %copy-start.4 = (f32[8,2,8,32,32]{3,4,2,1,0:T(8,128)S(1)}, f32[8,2,8,32,32]{3,4,2,1,0:T(8,128)}, u32[]{:S(2)}) copy-start(f32[8,2,8,32,32]{3,4,2,1,0:T(8,128)} %copy-done.2) | copy-start | bytes 1572868
  179.1 7.4 %copy-start.7 = (bf16[2,128,16,128]{3,2,1,0:T(8,128)(2,1)S(1)}, bf16[2,128,16,128]{3,2,1,0:T(8,128)(2,1)}, u32[]{:S(2)}) copy-start(bf16[2,128,16,128]{3,2,1,0:T(8,128)(2,1)} %copy-done.6) | copy-start | bytes 3145732
  179.1 19.6 %all-to-all-start.4 = ((bf16[256,16,128]{2,1,0:T(8,128)(2,1)}), bf16[256,16,128]{2,1,0:T(8,128)(2,1)}, u32[]{:S(2)}, u32[]{:S(2)}) async-start(bf16[256,16,128]{2,1,0:T(8,128)(2,1)} %bitcast.252), calls=%async_computation.4 | async-start | bytes 2097152 | tf_op jit(solution)/shard_map/all_to_all | solution.py:167
  187.3 22.6 %copy-start.15 = (bf16[256,16,128]{2,1,0:T(8,128)(2,1)S(1)}, bf16[256,16,128]{2,1,0:T(8,128)(2,1)}, u32[]{:S(2)}) copy-start(bf16[256,16,128]{2,1,0:T(8,128)(2,1)} %copy-done.14) | copy-start | bytes 3145732
  198.7 7.8 %all-to-all-start.9 = ((bf16[256,2,128]{2,1,0:T(2,128)(2,1)}), bf16[256,2,128]{2,1,0:T(2,128)(2,1)S(1)}, u32[]{:S(2)}, u32[]{:S(2)}) async-start(bf16[256,2,128]{2,1,0:T(2,128)(2,1)} %copy.136), calls=%async_computation.9 | async-start | bytes 262144 | tf_op jit(solution)/shard_map/all_to_all | solution.py:172
  206.6 7.8 %all-to-all-start.8 = ((bf16[256,2,128]{2,1,0:T(2,128)(2,1)}), bf16[256,2,128]{2,1,0:T(2,128)(2,1)S(1)}, u32[]{:S(2)}, u32[]{:S(2)}) async-start(bf16[256,2,128]{2,1,0:T(2,128)(2,1)} %copy.131), calls=%async_computation.8 | async-start | bytes 262144 | tf_op jit(solution)/shard_map/all_to_all | solution.py:171
  (6 other events, 8.7 us)
where the time goes:
time: 217 us; the launch traced here: 215 us
  waiting for transfers between devices  60.3 us (28%)
  starting transfers between devices  35.9 us (17%)
  local copies, waits for them, and re-layouts  35.3 us (16%)
  matrix products  32.2 us (15%)
  blocking collectives  29.1 us (13%)
  other arithmetic  17.1 us (8%)
  loops' own time  4.02 us (2%)
    all_to_all x1, blocking collectives, on_device(): lax.all_to_all(far_grads, 'grp', split_axis=1, concat_axis=1, tiled=True)  29.1 us
    all_to_all x1, waiting for transfers between devices, on_device(): lax.all_to_all(query_rows, 'uly', split_axis=0, concat_axis=1, tiled=True)  13.9 us
    all_to_all x1, waiting for transfers between devices, on_device(): lax.all_to_all(queries, 'uly', split_axis=1, concat_axis=0, tiled=True)  12.9 us
    unnamed x57, local copies, waits for them, and re-layouts  12.2 us
    all_to_all x1, waiting for transfers between devices, on_device(): lax.all_to_all(attended_rows, 'uly', split_axis=0, concat_axis=1, tiled=T...  10.6 us
    all_to_all x1, waiting for transfers between devices, on_device(): lax.all_to_all(output_cotangent, 'uly', split_axis=1, concat_axis=0, tile...  9.72 us
    all_to_all x1, waiting for transfers between devices, on_device(): lax.all_to_all(outgoing, 'grp', split_axis=1, concat_axis=1, tiled=True)  7.02 us
    dot_general x2, matrix products, backward(): jnp.einsum('pkgqj,pjkd->pqkgd', dscores, key_rows, preferred_element_type...  5.96 us
  transfers between devices with their start and end apart: 9, of which 8 were waited for; matrix products, arithmetic and copies ran while one was open for 13% of the time, Pallas kernels for 0%

commit v1 on v0

--- a/solution.py
+++ b/solution.py
@@ -2,6 +2,29 @@
 import jax.numpy as jnp
 from jax import lax
 from jax.sharding import PartitionSpec as P
+
+
+def cut_along(array, dim, size):
+    before, after = (array.shape[:dim], array.shape[dim + 1 :])
+    return jnp.moveaxis(array.reshape(*before, size, -1, *after), dim, 0)
+
+
+def joined_along(blocks, dim):
+    shape = list(blocks.shape[1:])
+    shape[dim] *= blocks.shape[0]
+    return jnp.moveaxis(blocks, 0, dim).reshape(shape)
+
+
+def rotated_exchange(shard, axis, split_dim, concat_dim):
+    size, index = (lax.axis_size(axis), lax.axis_index(axis))
+    tiles = cut_along(shard, split_dim, size)
+    filled = tiles
+    for step in range(1, size):
+        target, source = ((index + step) % size, (index - step) % size)
+        sent = lax.dynamic_index_in_dim(tiles, target, 0)
+        received = lax.ppermute(sent, axis, [(i, (i + step) % size) for i in range(size)])
+        filled = lax.dynamic_update_slice_in_dim(filled, received, source, axis=0)
+    return joined_along(filled, concat_dim)
 
 
 def on_device(queries, keys, values, output_cotangent, block_lists, list_counts):
@@ -40,7 +63,7 @@
     )
     stacked = jnp.stack([to_blocks(key_heads), to_blocks(value_heads)])
     outgoing = jnp.take(stacked, send_place, axis=1)
-    arrived = lax.all_to_all(outgoing, "grp", split_axis=1, concat_axis=1, tiled=True)
+    arrived = rotated_exchange(outgoing, "grp", 1, 1)
     kv_local = key_heads.shape[1]
     heads_local = query_heads.shape[1]
     heads_per_group = heads_local // kv_local

time: 217 us -> 205 us (0.945)
  waiting for transfers between devices: 60.3 us -> 34.1 us
  starting transfers between devices: 35.9 us -> 53.9 us
  other arithmetic: 17.1 us -> 14.5 us
  local copies, waits for them, and re-layouts: 35.3 us -> 33.1 us
    ppermute x0 -> x15, starting transfers between devices: none -> 23 us  [rotated_exchange(): lax.ppermute(sent, axis, [(i, (i + step) % size) for i in range(size)])]
    all_to_all x1, waiting for transfers between devices: 12.9 us -> 0.01 us  [on_device(): lax.all_to_all(queries, 'uly', split_axis=1, concat_axis=0, tiled=True)]
    all_to_all x1, waiting for transfers between devices: 9.72 us -> 0.01 us  [on_device(): lax.all_to_all(output_cotangent, 'uly', split_axis=1, concat_axis=0, tile...]
    all_to_all x1 -> x0, waiting for transfers between devices: 7.02 us -> none  [on_device(): lax.all_to_all(outgoing, 'grp', split_axis=1, concat_axis=1, tiled=True)]
    all_to_all x1 -> x0, starting transfers between devices: 5.91 us -> none  [on_device(): lax.all_to_all(outgoing, 'grp', split_axis=1, concat_axis=1, tiled=True)]
    ppermute x0 -> x15, waiting for transfers between devices: none -> 2.17 us  [rotated_exchange(): lax.ppermute(sent, axis, [(i, (i + step) % size) for i in range(size)])]
    unnamed x57 -> x53, local copies, waits for them, and re-layouts: 12.2 us -> 11.6 us
  transfers between devices with their start and end apart: 9 -> 23, of which waited for: 8 -> 8; matrix products, arithmetic and copies ran while one was open for 13% -> 21% of each run, Pallas kernels for 0% -> 0%
where the time goes in v1:
time: 205 us; the launch traced here: 203 us
  starting transfers between devices  53.9 us (26%)
  waiting for transfers between devices  34.1 us (17%)
  matrix products  33.2 us (16%)
  local copies, waits for them, and re-layouts  33.1 us (16%)
  blocking collectives  28.3 us (14%)
  other arithmetic  14.5 us (7%)
  loops' own time  4.56 us (2%)
    all_to_all x1, blocking collectives, on_device(): lax.all_to_all(far_grads, 'grp', split_axis=1, concat_axis=1, tiled=True)  28.3 us
    ppermute x15, starting transfers between devices, rotated_exchange(): lax.ppermute(sent, axis, [(i, (i + step) % size) for i in range(size)])  23 us
    all_to_all x1, waiting for transfers between devices, on_device(): lax.all_to_all(query_rows, 'uly', split_axis=0, concat_axis=1, tiled=True)  14.9 us
    unnamed x53, local copies, waits for them, and re-layouts  11.6 us
    all_to_all x1, waiting for transfers between devices, on_device(): lax.all_to_all(attended_rows, 'uly', split_axis=0, concat_axis=1, tiled=T...  10.9 us
    dot_general x2, matrix products, backward(): jnp.einsum('pkgqj,pjkd->pqkgd', dscores, key_rows, preferred_element_type...  6.01 us
    dot_general x2, matrix products, backward(): jnp.einsum('pqkgd,pjkd->pkgqj', grad_blk, value_rows, preferred_element_t...  5.95 us
    all_to_all x1, starting transfers between devices, on_device(): lax.all_to_all(attended_rows, 'uly', split_axis=0, concat_axis=1, tiled=T...  4.67 us
  transfers between devices with their start and end apart: 23, of which 8 were waited for; matrix products, arithmetic and copies ran while one was open for 21% of the time, Pallas kernels for 0%

profile of v1, /device:TPU:0, one launch (start us, length us, event | category | flops | bytes accessed | tf_op | source)
XLA Modules:
  0.0 203.3 jit_solution(1031826136042258339)
XLA Ops:
  2.4 4.2 %all-to-all-start = ((bf16[128,4,128]{2,0,1:T(8,128)(2,1)}), bf16[128,4,128]{2,0,1:T(8,128)(2,1)S(1)}, u32[]{:S(2)}, u32[]{:S(2)}) async-start(bf16[128,4,128]{2,0,1:T(8,128)(2,1)} %copy.90), calls=%async_computation | async-start | bytes 262144 | tf_op jit(solution)/shard_map/all_to_all | solution.py:61
  15.0 3.6 %all-to-all-start.2 = ((bf16[128,4,128]{2,0,1:T(8,128)(2,1)}), bf16[128,4,128]{2,0,1:T(8,128)(2,1)S(1)}, u32[]{:S(2)}, u32[]{:S(2)}) async-start(bf16[128,4,128]{2,0,1:T(8,128)(2,1)} %copy.98), calls=%async_computation.2 | async-start | bytes 262144 | tf_op jit(solution)/shard_map/all_to_all | solution.py:62
  18.6 4.5 %all-to-all-done.2 = bf16[128,4,128]{2,0,1:T(8,128)(2,1)S(1)} async-done(((bf16[128,4,128]{2,0,1:T(8,128)(2,1)}), bf16[128,4,128]{2,0,1:T(8,128)(2,1)S(1)}, u32[]{:S(2)}, u32[]{:S(2)}) %all-to-all-start.2) | async-done | bytes 131104 | tf_op jit(solution)/shard_map/all_to_all | solution.py:62
  23.1 3.6 %all-to-all-start.1 = ((bf16[128,32,128]{2,0,1:T(8,128)(2,1)}), bf16[128,32,128]{2,0,1:T(8,128)(2,1)S(1)}, u32[]{:S(2)}, u32[]{:S(2)}) async-start(bf16[128,32,128]{2,0,1:T(8,128)(2,1)} %copy.92), calls=%async_computation.1 | async-start | bytes 2097152 | tf_op jit(solution)/shard_map/all_to_all | solution.py:59
  30.6 2.5 %collective-permute-start.2 = (bf16[1,2,1,32,2,128]{5,3,4,1,0,2:T(8,128)(2,1)S(1)}, bf16[1,2,1,32,2,128]{5,3,4,1,0,2:T(8,128)(2,1)S(1)}, u32[]{:S(2)}, u32[]{:S(2)}) collective-permute-start(bf16[1,2,1,32,2,128]{5,3,4,1,0,2:T(8,128)(2,1)S(1)} %get-tuple-element.642), channel_id=1, source_target_pairs={{0,6},{2,8},{4,10},{6,12},{8,14},{10,16},{12,18},{14,20},{16,22},{... | collective-permute-start | bytes 98312 | tf_op jit(solution)/shard_map/ppermute | solution.py:25
  36.1 4.4 %collective-permute-start.6 = (bf16[1,2,1,32,2,128]{5,3,4,1,0,2:T(8,128)(2,1)S(1)}, bf16[1,2,1,32,2,128]{5,3,4,1,0,2:T(8,128)(2,1)S(1)}, u32[]{:S(2)}, u32[]{:S(2)}) collective-permute-start(bf16[1,2,1,32,2,128]{5,3,4,1,0,2:T(8,128)(2,1)S(1)} %get-tuple-element.638), channel_id=1, source_target_pairs={{0,14},{2,16},{4,18},{6,20},{8,22},{10,24},{12,26},{14,28},{16,30}... | collective-permute-start | bytes 98312 | tf_op jit(solution)/shard_map/ppermute | solution.py:25
  43.6 2.9 %collective-permute-start.10 = (bf16[1,2,1,32,2,128]{5,3,4,1,0,2:T(8,128)(2,1)S(1)}, bf16[1,2,1,32,2,128]{5,3,4,1,0,2:T(8,128)(2,1)S(1)}, u32[]{:S(2)}, u32[]{:S(2)}) collective-permute-start(bf16[1,2,1,32,2,128]{5,3,4,1,0,2:T(8,128)(2,1)S(1)} %get-tuple-element.634), channel_id=1, source_target_pairs={{0,22},{2,24},{4,26},{6,28},{8,30},{10,0},{12,2},{14,4},{16,6},{18... | collective-permute-start | bytes 98312 | tf_op jit(solution)/shard_map/ppermute | solution.py:25
  50.1 2.3 %collective-permute-start.14 = (bf16[1,2,1,32,2,128]{5,3,4,1,0,2:T(8,128)(2,1)S(1)}, bf16[1,2,1,32,2,128]{5,3,4,1,0,2:T(8,128)(2,1)S(1)}, u32[]{:S(2)}, u32[]{:S(2)}) collective-permute-start(bf16[1,2,1,32,2,128]{5,3,4,1,0,2:T(8,128)(2,1)S(1)} %get-tuple-element.630), channel_id=1, source_target_pairs={{0,30},{2,0},{4,2},{6,4},{8,6},{10,8},{12,10},{14,12},{16,14},{18,... | collective-permute-start | bytes 98312 | tf_op jit(solution)/shard_map/ppermute | solution.py:25
  55.3 4.4 %all-to-all-start.4 = ((bf16[128,32,128]{2,0,1:T(8,128)(2,1)}), bf16[128,32,128]{2,0,1:T(8,128)(2,1)}, u32[]{:S(2)}, u32[]{:S(2)}) async-start(bf16[128,32,128]{2,0,1:T(8,128)(2,1)} %copy.110), calls=%async_computation.4 | async-start | bytes 2097152 | tf_op jit(solution)/shard_map/all_to_all | solution.py:60
  63.5 3.0 %copy.103 = f32[8,2,32,32,8]{3,4,2,1,0:T(8,128)} copy(f32[8,2,32,32,8]{3,2,4,1,0:T(8,128)S(1)} %fusion.57) | data formatting | bytes 1048576 | tf_op jit(solution)/shard_map/while | solution.py:111
  68.5 2.7 %fusion.97 = (f32[8,2,8,32]{3,2,1,0:T(8,128)S(1)}, f32[8,2,8,32,32]{3,4,2,1,0:T(8,128)S(1)}) fusion(bf16[8,32,2,8,128]{4,3,2,1,0:T(8,128)(2,1)S(1)} %bitcast.282, bf16[8,32,2,128,1]{3,1,0,2,4:T(8,128)(2,1)} %bitcast.289, pred[32,32]{0,1:T(8,128)(4,1)S(1)} %iota_compare_fusion), kind=kOutput, calls=%fused_computation.182 | convolution fusion | flops 33943552 | bytes 1721344 | tf_op jit(solution)/shard_map/pqkgd,pjkd->pkgqj/dot_general | solution.py:80
  73.2 4.2 %while.43 = (s32[]{:T(128)}, f32[8,2,8,32]{3,2,1,0:T(8,128)S(1)}, f32[8,2,8,32]{3,2,1,0:T(8,128)S(1)}, s32[]{:T(128)}, pred[8,1]{0,1:T(4,128)(4,1)S(1)}, /*index=5*/f32[8,2,32,32,8]{3,4,2,1,0:T(8,128)}, s32[]{:T(128)}) while((s32[]{:T(128)}, f32[8,2,8,32]{3,2,1,0:T(8,128)S(1)}, f32[8,2,8,32]{3,2,1,0:T(8,128)S(1)}, s32[]{:T(128)}, ...), condition=%wide.region_7.9_spmd, body=%wide.region_4.8_spmd.sunk | while | flops 925698 | bytes 3358841 | solution.py:111
  77.4 3.5 %convolution_bitcast_fusion.1 = f32[8,32,2,8,128]{4,1,3,2,0:T(8,128)} fusion(f32[8,2,8,32,32]{3,4,2,1,0:T(8,128)} %copy-done.2, f32[8,2,8,32]{3,2,1,0:T(8,128)S(1)} %log_add_fusion, bf16[8,32,2,128,1]{3,1,0,2,4:T(8,128)(2,1)S(1)} %bitcast.292), kind=kOutput, calls=%fused_computation.52 | convolution fusion | flops 33816576 | bytes 2768896 | tf_op jit(solution)/shard_map/pkgqj,pjkd->pqkgd/dot_general | solution.py:117
  81.0 4.8 %while.44 = (s32[]{:T(128)}, f32[8,32,2,8,128]{4,1,3,2,0:T(8,128)}, s32[]{:T(128)}, pred[8,1]{0,1:T(4,128)(4,1)S(1)}, f32[8,2,32,32,8]{2,3,4,1,0:T(8,128)S(1)}, ...) while((s32[]{:T(128)}, f32[8,32,2,8,128]{4,1,3,2,0:T(8,128)}, s32[]{:T(128)}, ...), condition=%wide.region_9.11_spmd, body=%wide.region_8.10_spmd.sunk | while | flops 34603008 | bytes 4866141 | solution.py:131
  81.9 3.3 %bitcast_add_fusion.6 = f32[8,32,2,8,128]{4,1,3,2,0:T(8,128)} fusion(f32[8,32,2,8,128]{4,1,3,2,0:T(8,128)} %get-tuple-element.829, f32[8,2,32,32,8]{2,3,4,1,0:T(8,128)S(1)} %get-tuple-element.840, f32[8,2,8,32]{3,2,1,0:T(8,128)S(1)} %get-tuple-element.841, pred[8]{0:T(512)(128)(4,1)S(1)} %bitcast.310, bf16[8,32,2,128]{3,1,2,0:T(8,128)(2,1)S(1)} %get-tuple-element.842), kind=kOutput, calls=%fused_computation.9.clone.1 | convolution fusion | flops 34603008 | bytes 4866056 | tf_op jit(solution)/shard_map/while/body/pkgqj,pjkd->pqkgd/dot_general | solution.py:127
  87.8 3.2 %fusion.52 = f32[8,2,32,32,8]{3,2,4,1,0:T(8,128)} fusion(bf16[8,32,2,8,128]{4,3,2,1,0:T(8,128)(2,1)S(1)} %bitcast.276, bf16[8,32,2,128]{3,1,2,0:T(8,128)(2,1)S(1)} %get-tuple-element.883), kind=kOutput, calls=%fused_computation.76 | convolution fusion | flops 33554432 | bytes 1703936 | tf_op jit(solution)/shard_map/while/body/pqkgd,pjkd->pkgqj/dot_general | solution.py:141
  90.9 3.2 %multiply_reduce_fusion = (f32[8,32,2,8]{3,2,1,0:T(2,128)}, bf16[8,32,2,8,128]{4,3,2,1,0:T(8,128)(2,1)}) fusion(bf16[8,32,2,8,128]{4,3,2,1,0:T(8,128)(2,1)S(1)} %bitcast.277, f32[8,32,2,8,128]{4,1,3,2,0:T(8,128)S(1)} %copy-done.1), kind=kLoop, calls=%fused_computation.47 | loop fusion | flops 2093056 | bytes 4210688 | tf_op jit(solution)/shard_map/reduce_sum | solution.py:134
  95.2 3.3 %convolution_bitcast_fusion.4 = f32[1,8,32,2,128]{4,2,3,1,0:T(8,128)} fusion(f32[8,2,32,32,8]{3,2,4,1,0:T(8,128)} %copy-done.8, f32[8,2,8,32]{3,2,1,0:T(8,128)S(1)} %get-tuple-element.881, pred[8]{0:T(512)(128)(4,1)S(1)} %get-tuple-element.627, bf16[8,32,2,8,128]{4,3,2,1,0:T(8,128)(2,1)S(1)} %bitcast.278), kind=kOutput, calls=%fused_computation.56 | convolution fusion | flops 34078720 | bytes 1851400 | tf_op jit(solution)/shard_map/while/body/pkgqj,pqkgd->pjkd/dot_general | solution.py:152
  98.5 2.8 %fusion.28 = bf16[8,2,8,32,32]{3,4,2,1,0:T(8,128)(2,1)} fusion(f32[8,2,8,32,32]{3,4,2,1,0:T(8,128)S(1)} %copy-done.3, f32[8,2,8,32]{3,2,1,0:T(8,128)S(1)} %copy.115, f32[8,2,8,32]{3,2,1,0:T(8,128)S(1)} %get-tuple-element.881, bf16[8,32,2,8,128]{4,3,2,1,0:T(8,128)(2,1)S(1)} %bitcast.279, bf16[8,32,2,128,1]{3,1,0,2,4:T(8,128)(2,1)S(1)} %bitcast.293), kind=kOutput, calls=%fused_computation.42 | convolution fusion | flops 34078720 | bytes 1998848 | tf_op jit(solution)/shard_map/pqkgd,pjkd->pkgqj/dot_general | solution.py:141
  102.3 3.0 %copy.123 = f32[8,2,32,32,8]{2,3,4,1,0:T(8,128)} copy(f32[8,2,32,32,8]{3,2,4,1,0:T(8,128)} %fusion.52) | data formatting | bytes 1048576 | tf_op jit(solution)/shard_map/while | solution.py:177
  110.0 6.4 %while.45 = (s32[]{:T(128)}, f32[8,32,2,8,128]{4,1,3,2,0:T(8,128)}, f32[2,16,32,2,128]{4,3,2,1,0:T(2,128)S(1)}, s32[]{:T(128)}, pred[8,1]{0,1:T(4,128)(4,1)S(1)}...) while((s32[]{:T(128)}, f32[8,32,2,8,128]{4,1,3,2,0:T(8,128)}, ...), condition=%wide.region_12.14_spmd, body=%wide.region_11.13_spmd.sunk | while | flops 35127296 | bytes 12746905 | solution.py:177
  110.7 4.1 %bitcast_add_fusion.7 = f32[8,32,2,8,128]{4,1,3,2,0:T(8,128)} fusion(f32[8,32,2,8,128]{4,1,3,2,0:T(8,128)} %get-tuple-element.857, f32[8,2,32,32,8]{2,3,4,1,0:T(8,128)} %get-tuple-element.875, f32[8,2,32,32,8]{2,3,4,1,0:T(8,128)S(1)} %get-tuple-element.873, f32[8,2,8,32]{3,2,1,0:T(8,128)S(1)} %get-tuple-element.876, ...), kind=kOutput, calls=%fused_computation.20.clone.1 | convolution fusion | flops 34865152 | bytes 5406728 | tf_op jit(solution)/shard_map/while/body/pkgqj,pjkd->pqkgd/dot_general | solution.py:145
  116.4 3.9 %fusion.29 = bf16[8,32,2,8,128]{4,3,2,1,0:T(8,128)(2,1)} fusion(f32[8,32,2,8,128]{4,1,3,2,0:T(8,128)} %get-tuple-element.466), kind=kLoop, calls=%fused_computation.45 | loop fusion | flops 1048576 | bytes 3145728 | tf_op jit(solution)/shard_map/convert_element_type | solution.py:187
  120.4 3.6 %all-to-all-start.5 = ((bf16[256,16,128]{2,1,0:T(8,128)(2,1)}), bf16[256,16,128]{2,1,0:T(8,128)(2,1)S(1)}, u32[]{:S(2)}, u32[]{:S(2)}) async-start(bf16[256,16,128]{2,1,0:T(8,128)(2,1)} %bitcast.87), calls=%async_computation.5 | async-start | bytes 2097152 | tf_op jit(solution)/shard_map/all_to_all | solution.py:191
  124.0 14.9 %all-to-all-done.5 = bf16[256,16,128]{2,1,0:T(8,128)(2,1)S(1)} async-done(((bf16[256,16,128]{2,1,0:T(8,128)(2,1)}), bf16[256,16,128]{2,1,0:T(8,128)(2,1)S(1)}, u32[]{:S(2)}, u32[]{:S(2)}) %all-to-all-start.5) | async-done | bytes 1048608 | tf_op jit(solution)/shard_map/all_to_all | solution.py:191
  138.9 28.3 %all_to_all.119 = f32[2,16,32,2,128]{4,3,2,0,1:T(2,128)} all-to-all(f32[2,16,32,2,128]{4,3,2,0,1:T(2,128)S(1)} %copy.129), channel_id=1, replica_groups=mesh['grp'=16,'uly'=2] {'grp'}, dimensions={1} | all-to-all | bytes 2097152 | tf_op jit(solution)/shard_map/all_to_all | solution.py:181
  167.2 4.7 %all-to-all-start.3 = ((bf16[256,16,128]{2,1,0:T(8,128)(2,1)}), bf16[256,16,128]{2,1,0:T(8,128)(2,1)}, u32[]{:S(2)}, u32[]{:S(2)}) async-start(bf16[256,16,128]{2,1,0:T(8,128)(2,1)} %bitcast.285), calls=%async_computation.3 | async-start | bytes 2097152 | tf_op jit(solution)/shard_map/all_to_all | solution.py:190
  171.9 2.2 %fusion.39 = f32[2,32,2,128,8]{3,4,2,1,0:T(8,128)S(1)} fusion(f32[2,16,32,2,128]{4,3,2,0,1:T(2,128)} %all_to_all.119, s32[16]{0:T(128)S(1)} %fusion.72, pred[16]{0:T(512)(128)(4,1)S(1)} %get-tuple-element.620), kind=kOutput, calls=%fused_computation.64 | convolution fusion | flops 25166080 | bytes 1572944 | tf_op jit(solution)/shard_map/sp,xsjkd->xpjkd/dot_general | solution.py:182
  176.0 10.9 %all-to-all-done.3 = bf16[256,16,128]{2,1,0:T(8,128)(2,1)} async-done(((bf16[256,16,128]{2,1,0:T(8,128)(2,1)}), bf16[256,16,128]{2,1,0:T(8,128)(2,1)}, u32[]{:S(2)}, u32[]{:S(2)}) %all-to-all-start.3) | async-done | bytes 1048608 | tf_op jit(solution)/shard_map/all_to_all | solution.py:190
  186.8 3.4 %all-to-all-start.8 = ((bf16[256,2,128]{2,1,0:T(2,128)(2,1)}), bf16[256,2,128]{2,1,0:T(2,128)(2,1)S(1)}, u32[]{:S(2)}, u32[]{:S(2)}) async-start(bf16[256,2,128]{2,1,0:T(2,128)(2,1)} %copy.138), calls=%async_computation.8 | async-start | bytes 262144 | tf_op jit(solution)/shard_map/all_to_all | solution.py:195
  194.7 3.4 %all-to-all-start.7 = ((bf16[256,2,128]{2,1,0:T(2,128)(2,1)}), bf16[256,2,128]{2,1,0:T(2,128)(2,1)S(1)}, u32[]{:S(2)}, u32[]{:S(2)}) async-start(bf16[256,2,128]{2,1,0:T(2,128)(2,1)} %copy.133), calls=%async_computation.7 | async-start | bytes 262144 | tf_op jit(solution)/shard_map/all_to_all | solution.py:194
  199.2 2.4 %copy.109 = bf16[128,2,16,128]{3,2,1,0:T(8,128)(2,1)} copy(bf16[128,2,16,128]{3,2,0,1:T(8,128)(2,1)} %bitcast.62) | data formatting | bytes 2097152 | tf_op jit(solution)/shard_map/all_to_all | solution.py:190
  (162 shorter events, 55.1 us)
Async XLA Ops:
  0.6 10.9 %copy-start.22 = (bf16[128,32,128]{2,1,0:T(8,128)(2,1)S(1)}, bf16[128,32,128]{2,1,0:T(8,128)(2,1)}, u32[]{:S(2)}) copy-start(bf16[128,32,128]{2,1,0:T(8,128)(2,1)} %param.14) | copy-start | bytes 3145732
  0.6 12.3 %copy-start.23 = (bf16[128,32,128]{2,1,0:T(8,128)(2,1)S(1)}, bf16[128,32,128]{2,1,0:T(8,128)(2,1)}, u32[]{:S(2)}) copy-start(bf16[128,32,128]{2,1,0:T(8,128)(2,1)} %param.17) | copy-start | bytes 3145732
  2.4 12.6 %all-to-all-start = ((bf16[128,4,128]{2,0,1:T(8,128)(2,1)}), bf16[128,4,128]{2,0,1:T(8,128)(2,1)S(1)}, u32[]{:S(2)}, u32[]{:S(2)}) async-start(bf16[128,4,128]{2,0,1:T(8,128)(2,1)} %copy.90), calls=%async_computation | async-start | bytes 262144 | tf_op jit(solution)/shard_map/all_to_all | solution.py:61
  15.0 8.1 %all-to-all-start.2 = ((bf16[128,4,128]{2,0,1:T(8,128)(2,1)}), bf16[128,4,128]{2,0,1:T(8,128)(2,1)S(1)}, u32[]{:S(2)}, u32[]{:S(2)}) async-start(bf16[128,4,128]{2,0,1:T(8,128)(2,1)} %copy.98), calls=%async_computation.2 | async-start | bytes 262144 | tf_op jit(solution)/shard_map/all_to_all | solution.py:62
  18.6 8.2 %copy-start.16 = (bf16[2,128,2,128]{3,1,0,2:T(8,128)(2,1)}, bf16[2,128,2,128]{3,1,0,2:T(8,128)(2,1)S(1)}, u32[]{:S(2)}) copy-start(bf16[2,128,2,128]{3,1,0,2:T(8,128)(2,1)S(1)} %copy.91) | copy-start | bytes 393220
  23.1 32.1 %all-to-all-start.1 = ((bf16[128,32,128]{2,0,1:T(8,128)(2,1)}), bf16[128,32,128]{2,0,1:T(8,128)(2,1)S(1)}, u32[]{:S(2)}, u32[]{:S(2)}) async-start(bf16[128,32,128]{2,0,1:T(8,128)(2,1)} %copy.92), calls=%async_computation.1 | async-start | bytes 2097152 | tf_op jit(solution)/shard_map/all_to_all | solution.py:59
  28.4 6.4 %collective-permute-start = (bf16[1,2,1,32,2,128]{5,3,4,1,0,2:T(8,128)(2,1)S(1)}, bf16[1,2,1,32,2,128]{5,3,4,1,0,2:T(8,128)(2,1)S(1)}, u32[]{:S(2)}, u32[]{:S(2)}) collective-permute-start(bf16[1,2,1,32,2,128]{5,3,4,1,0,2:T(8,128)(2,1)S(1)} %get-tuple-element.644), channel_id=1, source_target_pairs={{0,2},{2,4},{4,6},{6,8},{8,10},{10,12},{12,14},{14,16},{16,18},{18... | collective-permute-start | bytes 98312 | tf_op jit(solution)/shard_map/ppermute | solution.py:25
  28.6 7.5 %collective-permute-start.1 = (bf16[1,2,1,32,2,128]{5,3,4,1,0,2:T(8,128)(2,1)S(1)}, bf16[1,2,1,32,2,128]{5,3,4,1,0,2:T(8,128)(2,1)S(1)}, u32[]{:S(2)}, u32[]{:S(2)}) collective-permute-start(bf16[1,2,1,32,2,128]{5,3,4,1,0,2:T(8,128)(2,1)S(1)} %get-tuple-element.643), channel_id=1, source_target_pairs={{0,4},{2,6},{4,8},{6,10},{8,12},{10,14},{12,16},{14,18},{16,20},{1... | collective-permute-start | bytes 98312 | tf_op jit(solution)/shard_map/ppermute | solution.py:25
  30.6 9.8 %collective-permute-start.2 = (bf16[1,2,1,32,2,128]{5,3,4,1,0,2:T(8,128)(2,1)S(1)}, bf16[1,2,1,32,2,128]{5,3,4,1,0,2:T(8,128)(2,1)S(1)}, u32[]{:S(2)}, u32[]{:S(2)}) collective-permute-start(bf16[1,2,1,32,2,128]{5,3,4,1,0,2:T(8,128)(2,1)S(1)} %get-tuple-element.642), channel_id=1, source_target_pairs={{0,6},{2,8},{4,10},{6,12},{8,14},{10,16},{12,18},{14,20},{16,22},{... | collective-permute-start | bytes 98312 | tf_op jit(solution)/shard_map/ppermute | solution.py:25
  33.1 7.8 %collective-permute-start.3 = (bf16[1,2,1,32,2,128]{5,3,4,1,0,2:T(8,128)(2,1)S(1)}, bf16[1,2,1,32,2,128]{5,3,4,1,0,2:T(8,128)(2,1)S(1)}, u32[]{:S(2)}, u32[]{:S(2)}) collective-permute-start(bf16[1,2,1,32,2,128]{5,3,4,1,0,2:T(8,128)(2,1)S(1)} %get-tuple-element.641), channel_id=1, source_target_pairs={{0,8},{2,10},{4,12},{6,14},{8,16},{10,18},{12,20},{14,22},{16,24},... | collective-permute-start | bytes 98312 | tf_op jit(solution)/shard_map/ppermute | solution.py:25
  34.7 7.2 %collective-permute-start.4 = (bf16[1,2,1,32,2,128]{5,3,4,1,0,2:T(8,128)(2,1)S(1)}, bf16[1,2,1,32,2,128]{5,3,4,1,0,2:T(8,128)(2,1)S(1)}, u32[]{:S(2)}, u32[]{:S(2)}) collective-permute-start(bf16[1,2,1,32,2,128]{5,3,4,1,0,2:T(8,128)(2,1)S(1)} %get-tuple-element.640), channel_id=1, source_target_pairs={{0,10},{2,12},{4,14},{6,16},{8,18},{10,20},{12,22},{14,24},{16,26}... | collective-permute-start | bytes 98312 | tf_op jit(solution)/shard_map/ppermute | solution.py:25
  34.8 8.9 %collective-permute-start.5 = (bf16[1,2,1,32,2,128]{5,3,4,1,0,2:T(8,128)(2,1)S(1)}, bf16[1,2,1,32,2,128]{5,3,4,1,0,2:T(8,128)(2,1)S(1)}, u32[]{:S(2)}, u32[]{:S(2)}) collective-permute-start(bf16[1,2,1,32,2,128]{5,3,4,1,0,2:T(8,128)(2,1)S(1)} %get-tuple-element.639), channel_id=1, source_target_pairs={{0,12},{2,14},{4,16},{6,18},{8,20},{10,22},{12,24},{14,26},{16,28}... | collective-permute-start | bytes 98312 | tf_op jit(solution)/shard_map/ppermute | solution.py:25
  36.1 10.5 %collective-permute-start.6 = (bf16[1,2,1,32,2,128]{5,3,4,1,0,2:T(8,128)(2,1)S(1)}, bf16[1,2,1,32,2,128]{5,3,4,1,0,2:T(8,128)(2,1)S(1)}, u32[]{:S(2)}, u32[]{:S(2)}) collective-permute-start(bf16[1,2,1,32,2,128]{5,3,4,1,0,2:T(8,128)(2,1)S(1)} %get-tuple-element.638), channel_id=1, source_target_pairs={{0,14},{2,16},{4,18},{6,20},{8,22},{10,24},{12,26},{14,28},{16,30}... | collective-permute-start | bytes 98312 | tf_op jit(solution)/shard_map/ppermute | solution.py:25
  40.4 8.0 %collective-permute-start.7 = (bf16[1,2,1,32,2,128]{5,3,4,1,0,2:T(8,128)(2,1)S(1)}, bf16[1,2,1,32,2,128]{5,3,4,1,0,2:T(8,128)(2,1)S(1)}, u32[]{:S(2)}, u32[]{:S(2)}) collective-permute-start(bf16[1,2,1,32,2,128]{5,3,4,1,0,2:T(8,128)(2,1)S(1)} %get-tuple-element.637), channel_id=1, source_target_pairs={{0,16},{2,18},{4,20},{6,22},{8,24},{10,26},{12,28},{14,30},{16,0},... | collective-permute-start | bytes 98312 | tf_op jit(solution)/shard_map/ppermute | solution.py:25
  40.9 7.7 %collective-permute-start.8 = (bf16[1,2,1,32,2,128]{5,3,4,1,0,2:T(8,128)(2,1)S(1)}, bf16[1,2,1,32,2,128]{5,3,4,1,0,2:T(8,128)(2,1)S(1)}, u32[]{:S(2)}, u32[]{:S(2)}) collective-permute-start(bf16[1,2,1,32,2,128]{5,3,4,1,0,2:T(8,128)(2,1)S(1)} %get-tuple-element.636), channel_id=1, source_target_pairs={{0,18},{2,20},{4,22},{6,24},{8,26},{10,28},{12,30},{14,0},{16,2},{... | collective-permute-start | bytes 98312 | tf_op jit(solution)/shard_map/ppermute | solution.py:25
  41.8 8.2 %collective-permute-start.9 = (bf16[1,2,1,32,2,128]{5,3,4,1,0,2:T(8,128)(2,1)S(1)}, bf16[1,2,1,32,2,128]{5,3,4,1,0,2:T(8,128)(2,1)S(1)}, u32[]{:S(2)}, u32[]{:S(2)}) collective-permute-start(bf16[1,2,1,32,2,128]{5,3,4,1,0,2:T(8,128)(2,1)S(1)} %get-tuple-element.635), channel_id=1, source_target_pairs={{0,20},{2,22},{4,24},{6,26},{8,28},{10,30},{12,0},{14,2},{16,4},{1... | collective-permute-start | bytes 98312 | tf_op jit(solution)/shard_map/ppermute | solution.py:25
  43.6 8.7 %collective-permute-start.10 = (bf16[1,2,1,32,2,128]{5,3,4,1,0,2:T(8,128)(2,1)S(1)}, bf16[1,2,1,32,2,128]{5,3,4,1,0,2:T(8,128)(2,1)S(1)}, u32[]{:S(2)}, u32[]{:S(2)}) collective-permute-start(bf16[1,2,1,32,2,128]{5,3,4,1,0,2:T(8,128)(2,1)S(1)} %get-tuple-element.634), channel_id=1, source_target_pairs={{0,22},{2,24},{4,26},{6,28},{8,30},{10,0},{12,2},{14,4},{16,6},{18... | collective-permute-start | bytes 98312 | tf_op jit(solution)/shard_map/ppermute | solution.py:25
  46.6 5.8 %collective-permute-start.11 = (bf16[1,2,1,32,2,128]{5,3,4,1,0,2:T(8,128)(2,1)S(1)}, bf16[1,2,1,32,2,128]{5,3,4,1,0,2:T(8,128)(2,1)S(1)}, u32[]{:S(2)}, u32[]{:S(2)}) collective-permute-start(bf16[1,2,1,32,2,128]{5,3,4,1,0,2:T(8,128)(2,1)S(1)} %get-tuple-element.633), channel_id=1, source_target_pairs={{0,24},{2,26},{4,28},{6,30},{8,0},{10,2},{12,4},{14,6},{16,8},{18,... | collective-permute-start | bytes 98312 | tf_op jit(solution)/shard_map/ppermute | solution.py:25
  48.5 3.9 %collective-permute-start.12 = (bf16[1,2,1,32,2,128]{5,3,4,1,0,2:T(8,128)(2,1)S(1)}, bf16[1,2,1,32,2,128]{5,3,4,1,0,2:T(8,128)(2,1)S(1)}, u32[]{:S(2)}, u32[]{:S(2)}) collective-permute-start(bf16[1,2,1,32,2,128]{5,3,4,1,0,2:T(8,128)(2,1)S(1)} %get-tuple-element.632), channel_id=1, source_target_pairs={{0,26},{2,28},{4,30},{6,0},{8,2},{10,4},{12,6},{14,8},{16,10},{18,... | collective-permute-start | bytes 98312 | tf_op jit(solution)/shard_map/ppermute | solution.py:25
  48.6 4.0 %collective-permute-start.13 = (bf16[1,2,1,32,2,128]{5,3,4,1,0,2:T(8,128)(2,1)S(1)}, bf16[1,2,1,32,2,128]{5,3,4,1,0,2:T(8,128)(2,1)S(1)}, u32[]{:S(2)}, u32[]{:S(2)}) collective-permute-start(bf16[1,2,1,32,2,128]{5,3,4,1,0,2:T(8,128)(2,1)S(1)} %get-tuple-element.631), channel_id=1, source_target_pairs={{0,28},{2,30},{4,0},{6,2},{8,4},{10,6},{12,8},{14,10},{16,12},{18,... | collective-permute-start | bytes 98312 | tf_op jit(solution)/shard_map/ppermute | solution.py:25
  50.1 3.9 %collective-permute-start.14 = (bf16[1,2,1,32,2,128]{5,3,4,1,0,2:T(8,128)(2,1)S(1)}, bf16[1,2,1,32,2,128]{5,3,4,1,0,2:T(8,128)(2,1)S(1)}, u32[]{:S(2)}, u32[]{:S(2)}) collective-permute-start(bf16[1,2,1,32,2,128]{5,3,4,1,0,2:T(8,128)(2,1)S(1)} %get-tuple-element.630), channel_id=1, source_target_pairs={{0,30},{2,0},{4,2},{6,4},{8,6},{10,8},{12,10},{14,12},{16,14},{18,... | collective-permute-start | bytes 98312 | tf_op jit(solution)/shard_map/ppermute | solution.py:25
  55.3 30.6 %all-to-all-start.4 = ((bf16[128,32,128]{2,0,1:T(8,128)(2,1)}), bf16[128,32,128]{2,0,1:T(8,128)(2,1)}, u32[]{:S(2)}, u32[]{:S(2)}) async-start(bf16[128,32,128]{2,0,1:T(8,128)(2,1)} %copy.110), calls=%async_computation.4 | async-start | bytes 2097152 | tf_op jit(solution)/shard_map/all_to_all | solution.py:60
  60.4 8.1 %copy-start.10 = (bf16[2,128,16,128]{3,2,1,0:T(8,128)(2,1)}, bf16[2,128,16,128]{3,2,1,0:T(8,128)(2,1)S(1)}, u32[]{:S(2)}) copy-start(bf16[2,128,16,128]{3,2,1,0:T(8,128)(2,1)S(1)} %copy.94) | copy-start | bytes 3145732
  87.7 10.7 %copy-start.6 = (bf16[2,128,16,128]{3,2,1,0:T(8,128)(2,1)}, bf16[2,128,16,128]{3,2,1,0:T(8,128)(2,1)S(1)}, u32[]{:S(2)}) copy-start(bf16[2,128,16,128]{3,2,1,0:T(8,128)(2,1)S(1)} %copy.112) | copy-start | bytes 3145732
  120.4 18.6 %all-to-all-start.5 = ((bf16[256,16,128]{2,1,0:T(8,128)(2,1)}), bf16[256,16,128]{2,1,0:T(8,128)(2,1)S(1)}, u32[]{:S(2)}, u32[]{:S(2)}) async-start(bf16[256,16,128]{2,1,0:T(8,128)(2,1)} %bitcast.87), calls=%async_computation.5 | async-start | bytes 2097152 | tf_op jit(solution)/shard_map/all_to_all | solution.py:191
  138.9 28.3 %copy-start.14 = (bf16[256,16,128]{2,1,0:T(8,128)(2,1)}, bf16[256,16,128]{2,1,0:T(8,128)(2,1)S(1)}, u32[]{:S(2)}) copy-start(bf16[256,16,128]{2,1,0:T(8,128)(2,1)S(1)} %all-to-all-done.5) | copy-start | bytes 3145732
  167.2 7.1 %copy-start.4 = (f32[8,2,8,32,32]{3,4,2,1,0:T(8,128)S(1)}, f32[8,2,8,32,32]{3,4,2,1,0:T(8,128)}, u32[]{:S(2)}) copy-start(f32[8,2,8,32,32]{3,4,2,1,0:T(8,128)} %copy-done.2) | copy-start | bytes 1572868
  167.2 7.1 %copy-start.7 = (bf16[2,128,16,128]{3,2,1,0:T(8,128)(2,1)S(1)}, bf16[2,128,16,128]{3,2,1,0:T(8,128)(2,1)}, u32[]{:S(2)}) copy-start(bf16[2,128,16,128]{3,2,1,0:T(8,128)(2,1)} %copy-done.6) | copy-start | bytes 3145732
  167.2 19.6 %all-to-all-start.3 = ((bf16[256,16,128]{2,1,0:T(8,128)(2,1)}), bf16[256,16,128]{2,1,0:T(8,128)(2,1)}, u32[]{:S(2)}, u32[]{:S(2)}) async-start(bf16[256,16,128]{2,1,0:T(8,128)(2,1)} %bitcast.285), calls=%async_computation.3 | async-start | bytes 2097152 | tf_op jit(solution)/shard_map/all_to_all | solution.py:190
  175.2 22.9 %copy-start.15 = (bf16[256,16,128]{2,1,0:T(8,128)(2,1)S(1)}, bf16[256,16,128]{2,1,0:T(8,128)(2,1)}, u32[]{:S(2)}) copy-start(bf16[256,16,128]{2,1,0:T(8,128)(2,1)} %copy-done.14) | copy-start | bytes 3145732
  186.8 7.8 %all-to-all-start.8 = ((bf16[256,2,128]{2,1,0:T(2,128)(2,1)}), bf16[256,2,128]{2,1,0:T(2,128)(2,1)S(1)}, u32[]{:S(2)}, u32[]{:S(2)}) async-start(bf16[256,2,128]{2,1,0:T(2,128)(2,1)} %copy.138), calls=%async_computation.8 | async-start | bytes 262144 | tf_op jit(solution)/shard_map/all_to_all | solution.py:195
  194.7 7.8 %all-to-all-start.7 = ((bf16[256,2,128]{2,1,0:T(2,128)(2,1)}), bf16[256,2,128]{2,1,0:T(2,128)(2,1)S(1)}, u32[]{:S(2)}, u32[]{:S(2)}) async-start(bf16[256,2,128]{2,1,0:T(2,128)(2,1)} %copy.133), calls=%async_computation.7 | async-start | bytes 262144 | tf_op jit(solution)/shard_map/all_to_all | solution.py:194
  (16 other events, 44.1 us)
